TPU v7x, 768 devices: a whole 4x8x12 slice. The times are simulated.
768 devices in a mesh: row: 32 (over y, z_hi, core), col: 24 (over x, z_lo).
Axes of the slice: x: 4, y: 8, z: 12 (z_hi: 2, z_lo: 6; z = z_hi * 6 + z_lo), core: 2. Of those that a mesh axis runs over, the one named last changes fastest.
Arguments:
- a_tiles: bfloat16 [98304, 128, 128], P(('row', 'col')), may hold values from -6 to 6
- a_row: int32 [98304], P(('row', 'col')), may hold values from 0 to 95
- a_col: int32 [98304], P(('row', 'col')), may hold values from 0 to 11
- a_count: int32 [768], P(('row', 'col')), may hold values from 32 to 128
- p_tiles: bfloat16 [3072, 128, 128], P(('row', 'col')), may hold values from -0.5 to 0.5
Outputs:
- coarse_tiles: bfloat16 [1536, 128, 128], P(('row', 'col'))
All inputs are finite; a program needn't handle non-finite values.
Results may differ from a plain program's by a relative error of at most 0.0049.
Values may be sent and summed in bfloat16 or wider, within the bound.
A program may use at most 32 MiB of HBM per device.

v0:
```python
import math

import jax
import jax.numpy as jnp
from jax import lax
from jax.sharding import PartitionSpec as P


def shifted(block, axis, distance):
    devices = range(lax.axis_size(axis))
    route = [((i - distance) % len(devices), i) for i in devices]
    return lax.ppermute(block, axis, route)


def shards(a_tiles, a_row, a_col, a_count, p_tiles):
    tile_slots = a_tiles.shape[0]
    width = a_tiles.shape[1]
    held_blocks = p_tiles.shape[0]
    coarse_total = 3 * held_blocks * held_blocks
    block_size = math.gcd(tile_slots, 32)
    row_side = lax.all_gather(p_tiles, "col", axis=0, tiled=True)
    lower = shifted(p_tiles, "row", 1)
    upper = shifted(p_tiles, "row", -1)
    col_side = jnp.concatenate([lower, p_tiles, upper], axis=0)
    count = a_count[0]

    def advance(block_index, accum):
        start = block_index * block_size
        tiles = lax.dynamic_slice_in_dim(a_tiles, start, block_size, 0)
        rows = lax.dynamic_slice_in_dim(a_row, start, block_size, 0)
        cols = lax.dynamic_slice_in_dim(a_col, start, block_size, 0)
        slots = rows % held_blocks * (3 * held_blocks) + cols
        is_live = start + jnp.arange(block_size, dtype=jnp.int32) < count
        right = jnp.take(col_side, cols, axis=0)
        image = jnp.einsum("tij,tjk->tik", tiles, right, preferred_element_type=jnp.float32).astype(
            jnp.bfloat16
        )
        left = jnp.take(row_side, rows, axis=0)
        terms = jnp.einsum("tji,tjk->tik", left, image, preferred_element_type=jnp.float32)
        terms = jnp.where(is_live[:, None, None], terms, jnp.float32(0.0))
        return accum.at[slots].add(terms)

    empty = jnp.zeros((coarse_total, width, width), jnp.float32)
    live_blocks = (count + block_size - 1) // block_size
    accum = lax.fori_loop(0, live_blocks, advance, empty)
    summed = lax.psum_scatter(accum, "col", scatter_dimension=0, tiled=True)
    return summed.astype(jnp.bfloat16)


def solution(mesh):
    in_specs = (
        P(("row", "col"), None, None),
        P(("row", "col")),
        P(("row", "col")),
        P(("row", "col")),
        P(("row", "col"), None, None),
    )
    out_specs = P(("row", "col"), None, None)
    return jax.shard_map(shards, mesh=mesh, in_specs=in_specs, out_specs=out_specs, check_vma=False)
```

profile of v0, /device:TPU:16, one launch (start us, length us, event | category | flops | bytes accessed | tf_op | source)
XLA Modules:
  0.0 424.2 jit_solution(10063362580681325141)
XLA Ops:
  6.5 0.7 all-gather.2.cloned.1.call-update
  7.3 1.9 collective-permute-start
  9.2 14.5 %collective-permute-start.1 = (bf16[4,128,128]{2,1,0:T(8,128)(2,1)}, bf16[4,128,128]{2,1,0:T(8,128)(2,1)S(1)}, u32[]{:S(2)}, u32[]{:S(2)}) collective-permute-start(bf16[4,128,128]{2,1,0:T(8,128)(2,1)} %param.11), channel_id=1, source_target_pairs={{24,0},{48,24},{72,48},{96,72},{120,96},{144,120},{168,144},{192,1... | collective-permute-start | bytes 393224 | tf_op jit(solution)/shard_map/ppermute | solution.py:12
  24.4 0.5 collective-permute-done
  24.8 3.3 collective-permute-done.1
  28.1 0.9 pad_maximum_fusion
  29.1 153.4 %all-gather.2.cloned.1.call-done = bf16[96,128,128]{2,1,0:T(8,128)(2,1)} async-done(((bf16[4,128,128]{2,1,0:T(8,128)(2,1)}), bf16[96,128,128]{2,1,0:T(8,128)(2,1)}) %all-gather.2.cloned.1.call-update) | async-done | bytes 3145744 | tf_op jit(solution)/shard_map/all_gather | solution.py:21
  182.4 0.4 broadcast_in_dim.66
  182.8 31.9 %while.12 = (s32[]{:T(128)}, f32[48,128,128]{2,1,0:T(8,128)S(1)}, s32[]{:T(128)}, s32[128]{0:T(128)S(1)}, s32[128]{0:T(128)S(1)}, /*index=5*/s32[]{:T(128)}, bf1...) while((s32[]{:T(128)}, f32[48,128,128]{2,1,0:T(8,128)S(1)}, ...), condition=%wide.region_2.3_spmd, body=%wide.region_0.2_spmd.sunk | while | flops 271059904 | bytes 15742275 | solution.py:45
  182.8 1.1 add_compare_fusion.2
  184.1 0.7 compare_and_fusion.3
  184.7 3.6 gather_fusion.1
  188.3 1.7 gather_fusion
  190.0 4.1 convolution_select_fusion.2
  194.1 4.7 %scatter_fusion = f32[48,128,128]{2,1,0:T(8,128)S(1)} fusion(f32[48,128,128]{2,1,0:T(8,128)S(1)} %get-tuple-element.225, s32[32]{0:T(128)S(1)} %compare_select_fusion.8, f32[32,128,128]{2,1,0:T(8,128)} %convolution_select_fusion.2), kind=kCustom, calls=%fused_computation.2.clone.1 | custom fusion | flops 524288 | bytes 6291584 | tf_op jit(solution)/shard_map/while/body/scatter-add | solution.py:41
  198.8 1.1 add_compare_fusion.2
  200.0 0.7 compare_and_fusion.3
  200.7 3.6 gather_fusion.1
  204.3 1.7 gather_fusion
  205.9 4.1 convolution_select_fusion.2
  210.1 4.7 %scatter_fusion = f32[48,128,128]{2,1,0:T(8,128)S(1)} fusion(f32[48,128,128]{2,1,0:T(8,128)S(1)} %get-tuple-element.225, s32[32]{0:T(128)S(1)} %compare_select_fusion.8, f32[32,128,128]{2,1,0:T(8,128)} %convolution_select_fusion.2), kind=kCustom, calls=%fused_computation.2.clone.1 | custom fusion | flops 524288 | bytes 6291584 | tf_op jit(solution)/shard_map/while/body/scatter-add | solution.py:41
  214.8 1.6 copy-done
  216.4 199.4 %reduce-scatter.2.cloned.1.call-done = f32[2,128,128]{2,1,0:T(8,128)} async-done(((f32[48,128,128]{2,1,0:T(8,128)}), f32[2,128,128]{2,1,0:T(8,128)}) %reduce-scatter.2.cloned.1.call-update) | async-done | bytes 131088 | tf_op jit(solution)/shard_map/reduce_scatter | solution.py:46
  415.8 1.5 convert_element_type.9
  (18 shorter events, 0.3 us)
Async XLA Ops:
  6.5 176.3 %copy-start.2 = (s32[128]{0:T(128)S(1)}, s32[128]{0:T(128)}, u32[]{:S(2)}) copy-start(s32[128]{0:T(128)} %param.9) | copy-start | bytes 1540
  6.5 176.3 %copy-start.1 = (s32[128]{0:T(128)S(1)}, s32[128]{0:T(128)}, u32[]{:S(2)}) copy-start(s32[128]{0:T(128)} %param.8) | copy-start | bytes 1540
  6.5 175.9 %all-gather.2.cloned.1.call-start = ((), (), s32[]{:S(2)}) async-start(), calls=%async_computation.1 | async-start | bytes 3276800 | tf_op jit(solution)/shard_map/all_gather | solution.py:21
  7.3 408.6 %reduce-scatter.2.cloned.1.call-start = ((), (), s32[]{:S(2)}) async-start(), calls=%async_computation.2 | async-start | bytes 3276800 | tf_op jit(solution)/shard_map/reduce_scatter | solution.py:46
  7.3 17.5 %collective-permute-start = (bf16[4,128,128]{2,1,0:T(8,128)(2,1)}, bf16[4,128,128]{2,1,0:T(8,128)(2,1)S(1)}, u32[]{:S(2)}, u32[]{:S(2)}) collective-permute-start(bf16[4,128,128]{2,1,0:T(8,128)(2,1)} %param.11), channel_id=1, source_target_pairs={{744,0},{0,24},{24,48},{48,72},{72,96},{96,120},{120,144},{144,168... | collective-permute-start | bytes 393224 | tf_op jit(solution)/shard_map/ppermute | solution.py:12
  9.2 18.9 %collective-permute-start.1 = (bf16[4,128,128]{2,1,0:T(8,128)(2,1)}, bf16[4,128,128]{2,1,0:T(8,128)(2,1)S(1)}, u32[]{:S(2)}, u32[]{:S(2)}) collective-permute-start(bf16[4,128,128]{2,1,0:T(8,128)(2,1)} %param.11), channel_id=1, source_target_pairs={{24,0},{48,24},{72,48},{96,72},{120,96},{144,120},{168,144},{192,1... | collective-permute-start | bytes 393224 | tf_op jit(solution)/shard_map/ppermute | solution.py:12
  194.1 4.7 %copy-start.3 = (s32[128]{0:T(128)S(1)}, s32[128]{0:T(128)}, u32[]{:S(2)}) copy-start(s32[128]{0:T(128)} %get-tuple-element.275) | copy-start | bytes 1540 | tf_op jit(solution)/shard_map/while
  210.1 4.7 %copy-start.3 = (s32[128]{0:T(128)S(1)}, s32[128]{0:T(128)}, u32[]{:S(2)}) copy-start(s32[128]{0:T(128)} %get-tuple-element.275) | copy-start | bytes 1540 | tf_op jit(solution)/shard_map/while
  214.8 1.6 copy-start
Sparse Core Ops, SparseCore 0:
  9.8 172.6 all-gather.1
  216.5 199.2 reduce-scatter.1
where the time goes:
time: 425 us; the launch traced here: 424 us
  waiting for transfers between devices  357 us (84%)
  starting transfers between devices  16.4 us (4%)
  other arithmetic  15.6 us (4%)
  between operations  14.1 us (3%)
  local copies, waits for them, and re-layouts  12.5 us (3%)
  matrix products  8.22 us (2%)
    reduce_scatter x1, waiting for transfers between devices, shards(): summed = lax.psum_scatter(accum, 'col', scatter_dimension=0, tiled=True)  199 us
    all_gather x1, waiting for transfers between devices, shards(): row_side = lax.all_gather(p_tiles, 'col', axis=0, tiled=True)  153 us
    ppermute x2, starting transfers between devices, shifted(): return lax.ppermute(block, axis, route)  16.4 us
    scatter-add x2, other arithmetic, advance(): return accum.at[slots].add(terms)  9.34 us
  transfers between devices with their start and end apart: 4, of which 4 were waited for; matrix products, arithmetic and copies ran while one was open for 0% of the time, Pallas kernels for 0%

commit v1 on v0

v1 whole, which is shorter than its diff:
```python
import functools

import jax
import jax.numpy as jnp
from jax import lax
from jax.experimental import pallas as pl
from jax.experimental.pallas import tpu as pltpu
from jax.sharding import PartitionSpec as P

MESH = pl.DeviceIdType.MESH
F32 = jnp.float32
BF16 = jnp.bfloat16
NX, NZ = 4, 6


def kernel_body(
    n_row, pb, slots, width,
    acol_s, arow_s, acount_s, acol_v, arow_v, a_hbm, p_hbm, out_ref,
    abuf, colbuf, rowbuf, img, seg, tabv, tabs,
    sb1, rb1, sb2, rb2, red, zb, zr,
    a_sem, p_sem, t_sem, sh_send, sh_recv,
    z_send, z_recv, x_send, x_recv, y_send, y_recv,
    r1_send, r1_recv, r2_send, r2_recv, q_send, q_recv,
):
    row = lax.axis_index("row")
    col = lax.axis_index("col")
    x = col // NZ
    z = lax.rem(col, NZ)
    nc = 3 * pb
    up = (lax.rem(row + 1, n_row), col)
    down = (lax.rem(row + n_row - 1, n_row), col)
    xr = lax.rem(x + 1, NX)
    xl = lax.rem(x + NX - 1, NX)
    xf = lax.rem(x + 2, NX)
    right = (row, xr * NZ + z)
    left = (row, xl * NZ + z)
    zup = (row, x * NZ + lax.rem(z + 1, NZ))
    zdn = (row, x * NZ + lax.rem(z + NZ - 1, NZ))
    has_up = z < NZ - 1
    has_dn = z > 0

    def remote(src, dst, ssem, rsem, dev):
        return pltpu.make_async_remote_copy(
            src_ref=src, dst_ref=dst, send_sem=ssem, recv_sem=rsem,
            device_id=dev, device_id_type=MESH)

    own = colbuf.at[pl.ds(pb, pb)]
    p_copy = pltpu.make_async_copy(p_hbm, own, p_sem)
    p_copy.start()

    barrier = pltpu.get_barrier_semaphore()
    for dev in (right, left, up, down):
        pl.semaphore_signal(barrier, inc=1, device_id=dev, device_id_type=MESH)

    @pl.when(has_up)
    def _():
        pl.semaphore_signal(barrier, inc=1, device_id=zup, device_id_type=MESH)

    @pl.when(has_dn)
    def _():
        pl.semaphore_signal(barrier, inc=1, device_id=zdn, device_id_type=MESH)

    n_a = 4
    part = slots // n_a
    a_copies = []
    for i in range(n_a):
        c = pltpu.make_async_copy(
            a_hbm.at[pl.ds(i * part, part)], abuf.at[pl.ds(i * part, part)], a_sem.at[i])
        a_copies.append(c)

    p_copy.wait()
    for k in range(pb):
        rowbuf[col * pb + k] = colbuf[pb + k].T
    for c in a_copies:
        c.start()

    pl.semaphore_wait(barrier, 4 + has_up.astype(jnp.int32) + has_dn.astype(jnp.int32))

    def slot(xx, zz):
        return rowbuf.at[pl.ds((xx * NZ + zz) * pb, pb)]

    half = pb // 2

    def slot_half(xx, zz, h):
        return rowbuf.at[pl.ds((xx * NZ + zz) * pb + h * half, half)]

    def z_msg(direction, dist, zz):
        dev = zup if direction == 0 else zdn
        s = slot(x, zz)
        return remote(s, s, z_send.at[direction, dist], z_recv.at[direction, dist + 1], dev)

    def z_in(direction, dist, zz):
        s = slot(x, zz)
        return remote(s, s, z_send.at[direction, dist], z_recv.at[direction, dist], zup)

    def x_msg(direction, j, xx, zz):
        dev = right if direction == 0 else left
        s = slot(xx, zz)
        return remote(s, s, x_send.at[direction, j], x_recv.at[direction, j], dev)

    def y_msg(direction, j, xx, zz):
        dev = right if direction == 0 else left
        s = slot_half(xx, zz, direction)
        return remote(s, s, y_send.at[direction, j], y_recv.at[direction, j], dev)

    def when(cond, fn):
        if cond is None:
            fn()
        else:
            pl.when(cond)(fn)

    def entries(h):
        if h == 0:
            return [(0, z, None)]
        return [(h, z - h, z - h >= 0), (NZ - 1 + h, z + h, z + h < NZ)]

    def z_step(h):
        if h == 0:
            pl.when(has_up)(lambda: z_msg(0, 0, z).start())
            pl.when(has_dn)(lambda: z_msg(1, 0, z).start())
            x_msg(0, 0, x, z).start()
            x_msg(1, 0, x, z).start()
            return
        for side, (j, zz, there) in enumerate(entries(h)):
            def go(side=side, j=j, zz=zz):
                z_in(side, h, zz).wait_recv()
                if h < NZ - 1:
                    more = has_up if side == 0 else has_dn
                    pl.when(more)(lambda: z_msg(side, h, zz).start())
                x_msg(0, j, x, zz).start()
                x_msg(1, j, x, zz).start()
            pl.when(there)(go)

    def x_step(h):
        for j, zz, there in entries(h):
            def go(j=j, zz=zz):
                x_msg(0, j, xl, zz).wait_recv()
                y_msg(0, j, xl, zz).start()
                x_msg(1, j, xr, zz).wait_recv()
                y_msg(1, j, xr, zz).start()
            when(there, go)

    def y_step(h):
        for j, zz, there in entries(h):
            def go(j=j, zz=zz):
                y_msg(0, j, xf, zz).wait_recv()
                y_msg(1, j, xf, zz).wait_recv()
            when(there, go)

    def drain(h):
        for side, (j, zz, there) in enumerate(entries(h)):
            def go(side=side, j=j, zz=zz):
                if h == 0:
                    pl.when(has_up)(lambda: z_msg(0, 0, z).wait_send())
                    pl.when(has_dn)(lambda: z_msg(1, 0, z).wait_send())
                elif h < NZ - 1:
                    more = has_up if side == 0 else has_dn
                    pl.when(more)(lambda: z_msg(side, h, zz).wait_send())
                x_msg(0, j, x, zz).wait_send()
                x_msg(1, j, x, zz).wait_send()
                y_msg(0, j, xl, zz).wait_send()
                y_msg(1, j, xr, zz).wait_send()
            when(there, go)

    to_up = remote(own, colbuf.at[pl.ds(0, pb)], sh_send.at[0], sh_recv.at[0], up)
    to_dn = remote(own, colbuf.at[pl.ds(2 * pb, pb)], sh_send.at[1], sh_recv.at[1], down)

    z_step(0)
    to_up.start()
    to_dn.start()

    lane = lax.broadcasted_iota(jnp.int32, (slots, slots), 1)
    sub = lax.broadcasted_iota(jnp.int32, (slots, slots), 0)
    acol = jnp.broadcast_to(acol_v[...], (slots, slots))
    arow = jnp.broadcast_to(arow_v[...], (slots, slots))
    n_out = nc * pb
    key = jnp.where(lane < acount_s[0], (arow & (pb - 1)) * nc + acol, n_out)
    key_t = key.T
    before = (key_t < key) | ((key_t == key) & (sub < lane))
    rank = jnp.sum(before.astype(jnp.int32), axis=0, keepdims=True)
    rank_t = jnp.broadcast_to(rank, (slots, slots)).T
    hit = rank_t == lane
    order = jnp.sum(jnp.where(hit, sub, 0), axis=0, keepdims=True)
    s_key = jnp.sum(jnp.where(hit, key_t, 0), axis=0, keepdims=True)
    last = jnp.sum((key_t <= lane).astype(jnp.int32), axis=0, keepdims=True) - 1
    some = jnp.sum((key_t == lane).astype(jnp.int32), axis=0, keepdims=True)
    s_key8 = jnp.broadcast_to(s_key, (8, slots))
    prev = pltpu.roll(s_key8, 1, 1)
    lane8 = lax.broadcasted_iota(jnp.int32, (8, slots), 1)
    keep = jnp.where((lane8 > 0) & (prev == s_key8), 1, 0)
    sub8 = lax.broadcasted_iota(jnp.int32, (8, slots), 0)
    tabv[...] = jnp.where(
        sub8 == 0, jnp.broadcast_to(order, (8, slots)),
        jnp.where(sub8 == 1, keep,
                  jnp.where(sub8 == 2, jnp.broadcast_to(jnp.maximum(last, 0), (8, slots)),
                            jnp.broadcast_to(jnp.minimum(some, 1), (8, slots)))))
    t_copy = pltpu.make_async_copy(tabv, tabs, t_sem)
    t_copy.start()

    U = 8

    def images(first, count):
        def body(i, carry):
            for u in range(U):
                t = first + i * U + u
                img[t] = jnp.dot(abuf[t], colbuf[acol_s[t]],
                                 preferred_element_type=F32).astype(BF16)
            return carry
        lax.fori_loop(0, count // U, body, 0)

    z_step(1)
    x_step(0)
    z_step(2)
    x_step(1)
    to_up.wait_recv()
    to_dn.wait_recv()
    for c in a_copies:
        c.wait()
    images(0, 16)
    z_step(3)
    x_step(2)
    images(16, 16)
    z_step(4)
    x_step(3)
    images(32, 16)
    z_step(5)
    x_step(4)
    images(48, 40)
    x_step(5)
    images(88, 40)
    for h in range(NZ):
        y_step(h)
    t_copy.wait()

    def terms(i, carry):
        for u in range(U):
            p = i * U + u
            t = tabs[0, p]
            term = jnp.dot(rowbuf[arow_s[t]], img[t], preferred_element_type=F32)
            carry = carry * tabs[1, p].astype(F32) + term
            seg[p] = carry
        return carry
    lax.fori_loop(0, slots // U, terms, jnp.zeros((width, width), F32))

    def total(s):
        return seg[tabs[2, s]] * tabs[3, s].astype(F32)

    hc = nc // 2

    def each(n, fn):
        def body(i, carry):
            fn(i)
            return carry
        lax.fori_loop(0, n, body, 0)

    def fill1(a):
        sb1[0, a] = total(xf * nc + a).astype(BF16)
        sb1[1, a] = total(xf * nc + hc + a).astype(BF16)
    each(hc, fill1)
    r1r = remote(sb1.at[0], rb1.at[0], r1_send.at[0], r1_recv.at[0], right)
    r1l = remote(sb1.at[1], rb1.at[1], r1_send.at[1], r1_recv.at[1], left)
    r1r.start()
    r1l.start()

    def part2(direction, h, n):
        s = sb2.at[direction, pl.ds(h * hc, hc)]
        d = rb2.at[direction, pl.ds(h * hc, hc)]
        return remote(s, d, r2_send.at[n], r2_recv.at[n], right if direction == 0 else left)

    def fill2(a):
        sb2[0, hc + a] = total(xr * nc + hc + a).astype(BF16)
        sb2[1, a] = total(xl * nc + a).astype(BF16)
    each(hc, fill2)
    m2 = [part2(0, 1, 0), part2(1, 0, 1), part2(0, 0, 2), part2(1, 1, 3)]
    m2[0].start()
    m2[1].start()
    r1r.wait_recv()

    def fill3(a):
        sb2[0, a] = (total(xr * nc + a) + rb1[0, a].astype(F32)).astype(BF16)
    each(hc, fill3)
    m2[2].start()
    r1l.wait_recv()

    def fill4(a):
        sb2[1, hc + a] = (total(xl * nc + hc + a) + rb1[1, a].astype(F32)).astype(BF16)
    each(hc, fill4)
    m2[3].start()
    for m in m2:
        m.wait_recv()

    def reduce(a):
        v = total(x * nc + a) + rb2[0, a].astype(F32) + rb2[1, a].astype(F32)
        red[a] = v
        zb[a] = v.astype(BF16)
    each(nc, reduce)
    ct = nc // NZ
    m3 = []
    for d in range(1, NZ):
        zz = lax.rem(z + d, NZ)
        m = remote(zb.at[pl.ds(zz * ct, ct)], zr.at[d - 1],
                   q_send.at[d - 1], q_recv.at[d - 1], (row, x * NZ + zz))
        m.start()
        m3.append(m)
    for m in m3:
        m.wait_recv()
    for b in range(ct):
        v = red[z * ct + b]
        for d in range(NZ - 1):
            v = v + zr[d, b].astype(F32)
        out_ref[b] = v.astype(BF16)

    for h in range(NZ):
        drain(h)
    to_up.wait_send()
    to_dn.wait_send()
    for m in [r1r, r1l] + m2 + m3:
        m.wait_send()


def shards(a_tiles, a_row, a_col, a_count, p_tiles):
    slots, width = a_tiles.shape[0], a_tiles.shape[1]
    pb = p_tiles.shape[0]
    n_row = lax.axis_size("row")
    n_col = lax.axis_size("col")
    nc = 3 * pb
    ct = nc * pb // n_col
    hc = nc // 2
    tile = (width, width)
    vm = pltpu.VMEM
    dma = pltpu.SemaphoreType.DMA
    smem = pl.BlockSpec(memory_space=pltpu.SMEM)
    vmem = pl.BlockSpec(memory_space=pltpu.VMEM)
    hbm = pl.BlockSpec(memory_space=pl.ANY)
    nj = 2 * NZ - 1
    return pl.pallas_call(
        functools.partial(kernel_body, n_row, pb, slots, width),
        out_shape=jax.ShapeDtypeStruct((ct,) + tile, BF16),
        in_specs=[smem, smem, smem, vmem, vmem, hbm, hbm],
        out_specs=vmem,
        scratch_shapes=[
            vm((slots,) + tile, BF16),
            vm((nc,) + tile, BF16),
            vm((n_col * pb,) + tile, BF16),
            vm((slots,) + tile, BF16),
            vm((slots,) + tile, F32),
            vm((8, slots), jnp.int32),
            pltpu.SMEM((8, slots), jnp.int32),
            vm((2, hc) + tile, BF16),
            vm((2, hc) + tile, BF16),
            vm((2, nc) + tile, BF16),
            vm((2, nc) + tile, BF16),
            vm((nc,) + tile, F32),
            vm((nc,) + tile, BF16),
            vm((NZ - 1, ct) + tile, BF16),
            dma((4,)), dma(()), dma(()), dma((2,)), dma((2,)),
            dma((2, NZ)), dma((2, NZ)),
            dma((2, nj)), dma((2, nj)), dma((2, nj)), dma((2, nj)),
            dma((2,)), dma((2,)), dma((4,)), dma((4,)), dma((NZ - 1,)), dma((NZ - 1,)),
        ],
        compiler_params=pltpu.CompilerParams(
            collective_id=0, has_side_effects=True, vmem_limit_bytes=48 << 20),
    )(a_col, a_row, a_count, a_col.reshape(1, slots), a_row.reshape(1, slots), a_tiles, p_tiles)


def solution(mesh):
    in_specs = (
        P(("row", "col"), None, None),
        P(("row", "col")),
        P(("row", "col")),
        P(("row", "col")),
        P(("row", "col"), None, None),
    )
    out_specs = P(("row", "col"), None, None)
    return jax.shard_map(shards, mesh=mesh, in_specs=in_specs, out_specs=out_specs, check_vma=False)
```

time: 425 us -> 91.2 us (0.21)
  the two profiles are of different devices: /device:TPU:16 before, /device:TPU:32 now
where the time goes in v1:
time: 91.2 us; the launch traced here: 90.9 us
  Pallas kernels  85.3 us (94%)
  local copies, waits for them, and re-layouts  5.03 us (6%)
    pallas_call x1, Pallas kernels, shards(): pl.pallas_call(functools.partial(kernel_body, n_row, pb, slots, width), o...  85.3 us
    unnamed x9, local copies, waits for them, and re-layouts  5.03 us

profile of v1, /device:TPU:32, one launch (start us, length us, event | category | flops | bytes accessed | tf_op | source)
XLA Modules:
  0.0 90.9 jit_solution(3817450047700081250)
XLA Ops:
  0.7 0.0 copy-start
  0.7 2.2 %copy-done = bf16[128,128,128]{2,1,0:T(8,128)(2,1)S(1)} copy-done((bf16[128,128,128]{2,1,0:T(8,128)(2,1)S(1)}, bf16[128,128,128]{2,1,0:T(8,128)(2,1)}, u32[]{:S(2)}) %copy-start) | copy-done | bytes 4194328
  2.8 0.0 copy-start.1
  2.8 0.9 copy-done.1
  3.7 0.0 copy-start.2
  3.7 0.7 copy-done.2
  4.4 0.0 copy-start.3
  4.4 0.7 copy-done.3
  5.1 85.3 %shard_map.55 = bf16[2,128,128]{2,1,0:T(8,128)(2,1)S(1)} custom-call(s32[128]{0:T(128)S(1)} %copy-done.2, s32[128]{0:T(128)S(1)} %copy-done.3, s32[1]{0:T(128)S(6)} %copy.7.acount_s, s32[1,128]{1,0:T(1,128)S(1)} %bitcast.2, s32[1,128]{1,0:T(1,128)S(1)} %bitcast.3, bf16[128,128,128]{2,1,0:T(8,128)(2,1)S(1)} %copy-done, bf16[4,128,128]{2,1,0:T(8,128)(2,1)S(1)} %copy-done.1), custom_call_target="tpu_custom_call" | custom-call | tf_op jit(solution)/shard_map/pallas_call | solution.py:336
  90.3 0.6 copy.8
Async XLA Ops:
  0.7 2.2 %copy-start = (bf16[128,128,128]{2,1,0:T(8,128)(2,1)S(1)}, bf16[128,128,128]{2,1,0:T(8,128)(2,1)}, u32[]{:S(2)}) copy-start(bf16[128,128,128]{2,1,0:T(8,128)(2,1)} %a_hbm.1) | copy-start | bytes 12582916
  2.8 0.9 copy-start.1
  3.7 0.7 copy-start.2
  4.4 0.7 copy-start.3

commit v2 on v0

v2 whole, which is shorter than its diff:
```python
import functools

import jax
import jax.numpy as jnp
from jax import lax
from jax.experimental import pallas as pl
from jax.experimental.pallas import tpu as pltpu
from jax.sharding import PartitionSpec as P

MESH = pl.DeviceIdType.MESH
F32 = jnp.float32
BF16 = jnp.bfloat16
I32 = jnp.int32
NX, NZ, NQ = 4, 6, 2


def kernel_body(
    n_row, pb, slots, width,
    acol_s, arow_s, acount_s, acol_v, arow_v, a_hbm, p_hbm, out_ref,
    abuf, colbuf, row0, row1, img, seg0, seg1, tabv, tabs,
    fbuf, frecv, nbuf, nrecv, red, zb, zr,
    a_sem, p_sem, t_sem, sh_send, sh_recv,
    z_send, z_recv, x_send, x_recv, y_send, y_recv,
    f_send, f_recv, n_send, n_recv, q_send, q_recv,
):
    row = lax.axis_index("row")
    col = lax.axis_index("col")
    x = col // NZ
    z = lax.rem(col, NZ)
    core = lax.rem(row, 2)
    late = lax.rem(row // 2, 2)
    nc = 3 * pb
    rows = width // NQ
    rowb = (row0, row1)
    segs = (seg0, seg1)
    mate = (row + 1 - 2 * core, col)
    far = (lax.rem(row + n_row - 1 + 2 * core, n_row), col)
    mate_at = core * (2 * pb)
    far_at = (1 - core) * (2 * pb)
    xr = lax.rem(x + 1, NX)
    xl = lax.rem(x + NX - 1, NX)
    xf = lax.rem(x + 2, NX)
    right = (row, xr * NZ + z)
    left = (row, xl * NZ + z)
    has_up = z < NZ - 1
    has_dn = z > 0
    zup = (row, x * NZ + lax.rem(z + 1, NZ))
    zdn = (row, x * NZ + lax.rem(z + NZ - 1, NZ))

    def remote(src, dst, ssem, rsem, dev):
        return pltpu.make_async_remote_copy(
            src_ref=src, dst_ref=dst, send_sem=ssem, recv_sem=rsem,
            device_id=dev, device_id_type=MESH)

    def signal(dev):
        pl.semaphore_signal(pltpu.get_barrier_semaphore(), inc=1, device_id=dev, device_id_type=MESH)

    own = colbuf.at[pl.ds(pb, pb)]
    p_copy = pltpu.make_async_copy(p_hbm, own, p_sem)
    p_copy.start()
    barrier = pltpu.get_barrier_semaphore()
    for dev in (right, left, mate):
        signal(dev)
    pl.when(has_up)(lambda: signal(zup))
    pl.when(has_dn)(lambda: signal(zdn))

    p_copy.wait()
    for k in range(pb):
        flipped = colbuf[pb + k].T
        for q in range(NQ):
            rowb[q][col * pb + k] = flipped[q * rows:(q + 1) * rows]

    near = 3 + has_up.astype(I32) + has_dn.astype(I32)
    pl.semaphore_wait(barrier, near + late)
    signal(far)

    half = pb // 2

    def z_msg(q, zz, dev):
        s = rowb[q].at[pl.ds((x * NZ + zz) * pb, pb)]
        return remote(s, s, z_send.at[q, zz], z_recv.at[q, zz], dev)

    def z_both(q, side):
        s = rowb[q].at[pl.ds(col * pb, pb)]
        return remote(s, s, z_send.at[q, NZ + side], z_recv.at[q, z], zup if side == 0 else zdn)

    def x_msg(q, d, xx, zz):
        s = rowb[q].at[pl.ds((xx * NZ + zz) * pb, pb)]
        return remote(s, s, x_send.at[q, d, zz], x_recv.at[q, d, zz], right if d == 0 else left)

    def y_msg(q, d, xx, zz):
        s = rowb[q].at[pl.ds((xx * NZ + zz) * pb + d * half, half)]
        return remote(s, s, y_send.at[q, d, zz], y_recv.at[q, d, zz], right if d == 0 else left)

    pairs = jnp.minimum(z, NZ - 1 - z)
    more_below = z > NZ - 1 - z

    def place(n):
        if n == 0:
            return z
        side = (z - (n + 1) // 2) if n % 2 else (z + n // 2)
        rest = jnp.where(more_below, z - (n - pairs), z + (n - pairs))
        return jnp.where(n <= 2 * pairs, side, rest)

    def step(q, n):
        if n == 0:
            pl.when(has_up)(lambda: z_both(q, 0).start())
            pl.when(has_dn)(lambda: z_both(q, 1).start())
            x_msg(q, 0, x, z).start()
            x_msg(q, 1, x, z).start()
            return
        zz = place(n)
        z_msg(q, zz, zup).wait_recv()
        pl.when((zz < z) & has_up)(lambda: z_msg(q, zz, zup).start())
        pl.when((zz > z) & has_dn)(lambda: z_msg(q, zz, zdn).start())
        x_msg(q, 0, x, zz).start()
        x_msg(q, 1, x, zz).start()

    def relay(q, n):
        zz = place(n)
        x_msg(q, 0, xl, zz).wait_recv()
        y_msg(q, 0, xl, zz).start()
        x_msg(q, 1, xr, zz).wait_recv()
        y_msg(q, 1, xr, zz).start()

    def arrived(q):
        for n in range(NZ):
            zz = place(n)
            y_msg(q, 0, xf, zz).wait_recv()
            y_msg(q, 1, xf, zz).wait_recv()

    def drain(q):
        pl.when(has_up)(lambda: z_both(q, 0).wait_send())
        pl.when(has_dn)(lambda: z_both(q, 1).wait_send())
        for n in range(NZ):
            zz = place(n)
            if n > 0:
                pl.when((zz < z) & has_up)(lambda: z_msg(q, zz, zup).wait_send())
                pl.when((zz > z) & has_dn)(lambda: z_msg(q, zz, zdn).wait_send())
            for d in range(2):
                x_msg(q, d, x, zz).wait_send()
                y_msg(q, d, x, zz).wait_send()

    step(0, 0)
    to_mate = remote(own, colbuf.at[pl.ds(mate_at, pb)], sh_send.at[0], sh_recv.at[0], mate)
    to_far = remote(own, colbuf.at[pl.ds(far_at, pb)], sh_send.at[1], sh_recv.at[1], far)
    to_mate.start()
    step(1, 0)
    pl.when(late == 1)(lambda: to_far.start())

    n_a = 4
    part = slots // n_a
    a_copies = [
        pltpu.make_async_copy(
            a_hbm.at[pl.ds(i * part, part)], abuf.at[pl.ds(i * part, part)], a_sem.at[i])
        for i in range(n_a)]
    for c in a_copies:
        c.start()

    lane = lax.broadcasted_iota(I32, (slots, slots), 1)
    sub = lax.broadcasted_iota(I32, (slots, slots), 0)
    acol = jnp.broadcast_to(acol_v[...], (slots, slots))
    arow = jnp.broadcast_to(arow_v[...], (slots, slots))
    n_out = nc * pb
    key = jnp.where(lane < acount_s[0], (arow & (pb - 1)) * nc + acol, n_out)
    key_t = key.T
    before = (key_t < key) | ((key_t == key) & (sub < lane))
    rank = jnp.sum(before.astype(I32), axis=0, keepdims=True)
    rank_t = jnp.broadcast_to(rank, (slots, slots)).T
    hit = rank_t == lane
    order = jnp.sum(jnp.where(hit, sub, 0), axis=0, keepdims=True)
    s_key = jnp.sum(jnp.where(hit, key_t, 0), axis=0, keepdims=True)
    last = jnp.sum((key_t <= lane).astype(I32), axis=0, keepdims=True) - 1
    some = jnp.sum((key_t == lane).astype(I32), axis=0, keepdims=True)
    s_key8 = jnp.broadcast_to(s_key, (8, slots))
    prev = pltpu.roll(s_key8, 1, 1)
    lane8 = lax.broadcasted_iota(I32, (8, slots), 1)
    keep = jnp.where((lane8 > 0) & (prev == s_key8), 1, 0)
    sub8 = lax.broadcasted_iota(I32, (8, slots), 0)
    tabv[...] = jnp.where(
        sub8 == 0, jnp.broadcast_to(order, (8, slots)),
        jnp.where(sub8 == 1, keep,
                  jnp.where(sub8 == 2, jnp.broadcast_to(jnp.maximum(last, 0), (8, slots)),
                            jnp.broadcast_to(jnp.minimum(some, 1), (8, slots)))))
    t_copy = pltpu.make_async_copy(tabv, tabs, t_sem)
    t_copy.start()

    U = 8

    def images(first, count):
        def body(i, carry):
            for u in range(U):
                t = first + i * U + u
                img[t] = jnp.dot(abuf[t], colbuf[acol_s[t]],
                                 preferred_element_type=F32).astype(BF16)
            return carry
        lax.fori_loop(0, count // U, body, 0)

    def terms(q, first, count):
        def body(i, carry):
            for u in range(U):
                p = first + i * U + u
                t = tabs[0, p]
                term = jnp.dot(rowb[q][arow_s[t]], img[t], preferred_element_type=F32)
                carry = carry * tabs[1, p].astype(F32) + term
                segs[q][p] = carry
            return carry
        start = jnp.zeros((rows, width), F32) if first == 0 else segs[q][first - 1]
        lax.fori_loop(0, count // U, body, start)

    ct = nc // NZ

    def total(q, s):
        return segs[q][tabs[2, s]] * tabs[3, s].astype(F32)

    def group(d, i):
        return i if d == 0 else NZ - 1 - i

    def far_msg(q, d, i):
        return remote(fbuf.at[q, d, i], frecv.at[q, d, i], f_send.at[q, d, i], f_recv.at[q, d, i],
                      right if d == 0 else left)

    def near_msg(q, d, g):
        return remote(nbuf.at[q, d, g], nrecv.at[q, d, g], n_send.at[q, d, g], n_recv.at[q, d, g],
                      right if d == 0 else left)

    def z_out(q, g):
        return remote(zb.at[q, g], zr.at[q, z], q_send.at[q, g], q_recv.at[q, z], (row, x * NZ + g))

    def send_far(q, i):
        for d in range(2):
            for b in range(ct):
                fbuf[q, d, i, b] = total(q, xf * nc + group(d, i) * ct + b).astype(BF16)
            far_msg(q, d, i).start()

    def send_near(q, i):
        for d in range(2):
            g = group(1 - d, i)
            for b in range(ct):
                nbuf[q, d, g, b] = total(q, (xr if d == 0 else xl) * nc + g * ct + b).astype(BF16)
            near_msg(q, d, g).start()

    def send_joint(q, i):
        for d in range(2):
            g = group(d, i)
            far_msg(q, d, i).wait_recv()
            for b in range(ct):
                v = total(q, (xr if d == 0 else xl) * nc + g * ct + b)
                nbuf[q, d, g, b] = (v + frecv[q, d, i, b].astype(F32)).astype(BF16)
            near_msg(q, d, g).start()

    def finish(q, i):
        for g in (group(0, i), group(1, i)):
            near_msg(q, 0, g).wait_recv()
            near_msg(q, 1, g).wait_recv()
            for b in range(ct):
                v = total(q, x * nc + g * ct + b)
                v = v + nrecv[q, 0, g, b].astype(F32) + nrecv[q, 1, g, b].astype(F32)
                zb[q, g, b] = v.astype(BF16)

                def keep_own(v=v, b=b):
                    red[q, b] = v
                pl.when(z == g)(keep_own)
            pl.when(z != g)(lambda g=g: z_out(q, g).start())

    def z_in(q, zz):
        return remote(zb.at[q, 0], zr.at[q, zz], q_send.at[q, 0], q_recv.at[q, zz], zup)

    def close(q):
        for d in range(1, NZ):
            z_in(q, lax.rem(z + d, NZ)).wait_recv()
        for b in range(ct):
            v = red[q, b]
            for d in range(1, NZ):
                v = v + zr[q, lax.rem(z + d, NZ), b].astype(F32)
            out_ref[b, pl.ds(q * rows, rows)] = v.astype(BF16)

    def far_start():
        pl.semaphore_wait(barrier, 1)
        to_far.start()

    for n in range(1, NZ):
        step(0, n)
        step(1, n)
        if n >= 2:
            relay(0, n - 2)
            relay(1, n - 2)
        if n == NZ - 2:
            pl.when(late == 0)(far_start)
    to_mate.wait_recv()
    to_far.wait_recv()
    for c in a_copies:
        c.wait()
    images(0, 64)
    relay(0, NZ - 2)
    relay(1, NZ - 2)
    images(64, 64)
    relay(0, NZ - 1)
    relay(1, NZ - 1)
    t_copy.wait()
    arrived(0)
    terms(0, 0, slots)
    send_far(0, 0)
    send_far(0, 1)
    send_near(0, 0)
    send_joint(0, 0)
    send_far(0, 2)
    send_near(0, 1)
    send_joint(0, 1)
    send_near(0, 2)
    arrived(1)
    terms(1, 0, 64)
    send_joint(0, 2)
    terms(1, 64, 64)
    send_far(1, 0)
    send_far(1, 1)
    send_near(1, 0)
    finish(0, 0)
    send_joint(1, 0)
    finish(0, 1)
    send_far(1, 2)
    send_near(1, 1)
    send_joint(1, 1)
    finish(0, 2)
    send_near(1, 2)
    send_joint(1, 2)
    finish(1, 0)
    finish(1, 1)
    finish(1, 2)
    close(0)
    close(1)

    to_mate.wait_send()
    to_far.wait_send()
    for q in range(NQ):
        drain(q)
        for d in range(2):
            for i in range(NZ // 2):
                far_msg(q, d, i).wait_send()
            for g in range(NZ):
                near_msg(q, d, g).wait_send()
        for g in range(NZ):
            pl.when(z != g)(lambda g=g: z_out(q, g).wait_send())


def shards(a_tiles, a_row, a_col, a_count, p_tiles):
    slots, width = a_tiles.shape[0], a_tiles.shape[1]
    pb = p_tiles.shape[0]
    n_row = lax.axis_size("row")
    n_col = lax.axis_size("col")
    nc = 3 * pb
    ct = nc * pb // n_col
    tile = (width, width)
    part = (width // NQ, width)
    vm = pltpu.VMEM
    dma = pltpu.SemaphoreType.DMA
    smem = pl.BlockSpec(memory_space=pltpu.SMEM)
    vmem = pl.BlockSpec(memory_space=pltpu.VMEM)
    hbm = pl.BlockSpec(memory_space=pl.ANY)
    ng = NZ // 2
    return pl.pallas_call(
        functools.partial(kernel_body, n_row, pb, slots, width),
        out_shape=jax.ShapeDtypeStruct((ct,) + tile, BF16),
        in_specs=[smem, smem, smem, vmem, vmem, hbm, hbm],
        out_specs=vmem,
        scratch_shapes=[
            vm((slots,) + tile, BF16),
            vm((nc,) + tile, BF16),
            vm((n_col * pb,) + part, BF16),
            vm((n_col * pb,) + part, BF16),
            vm((slots,) + tile, BF16),
            vm((slots,) + part, F32),
            vm((slots,) + part, F32),
            vm((8, slots), I32),
            pltpu.SMEM((8, slots), I32),
            vm((NQ, 2, ng, ct) + part, BF16),
            vm((NQ, 2, ng, ct) + part, BF16),
            vm((NQ, 2, NZ, ct) + part, BF16),
            vm((NQ, 2, NZ, ct) + part, BF16),
            vm((NQ, ct) + part, F32),
            vm((NQ, NZ, ct) + part, BF16),
            vm((NQ, NZ, ct) + part, BF16),
            dma((4,)), dma(()), dma(()), dma((2,)), dma((2,)),
            dma((NQ, NZ + 2)), dma((NQ, NZ)),
            dma((NQ, 2, NZ)), dma((NQ, 2, NZ)), dma((NQ, 2, NZ)), dma((NQ, 2, NZ)),
            dma((NQ, 2, ng)), dma((NQ, 2, ng)), dma((NQ, 2, NZ)), dma((NQ, 2, NZ)),
            dma((NQ, NZ)), dma((NQ, NZ)),
        ],
        compiler_params=pltpu.CompilerParams(
            collective_id=0, has_side_effects=True, vmem_limit_bytes=67043328),
    )(a_col, a_row, a_count, a_col.reshape(1, slots), a_row.reshape(1, slots), a_tiles, p_tiles)


def solution(mesh):
    in_specs = (
        P(("row", "col"), None, None),
        P(("row", "col")),
        P(("row", "col")),
        P(("row", "col")),
        P(("row", "col"), None, None),
    )
    out_specs = P(("row", "col"), None, None)
    return jax.shard_map(shards, mesh=mesh, in_specs=in_specs, out_specs=out_specs, check_vma=False)
```

time: 425 us -> 75.2 us (0.18)
  the two profiles are of different devices: /device:TPU:16 before, /device:TPU:600 now
where the time goes in v2:
time: 75.2 us; the launch traced here: 75 us
  Pallas kernels  72.9 us (97%)
  local copies, waits for them, and re-layouts  1.47 us (2%)
    pallas_call x1, Pallas kernels, shards(): pl.pallas_call(functools.partial(kernel_body, n_row, pb, slots, width), o...  72.9 us

profile of v2, /device:TPU:600, one launch (start us, length us, event | category | flops | bytes accessed | tf_op | source)
XLA Modules:
  0.0 75.0 jit_solution(6549088586934766316)
XLA Ops:
  0.7 72.9 %shard_map.55 = bf16[2,128,128]{2,1,0:T(8,128)(2,1)} custom-call(s32[128]{0:T(128)} %acol_s.1, s32[128]{0:T(128)} %arow_s.1, s32[1]{0:T(128)S(6)} %copy.7.acount_s, s32[1,128]{1,0:T(1,128)} %bitcast.2, s32[1,128]{1,0:T(1,128)} %bitcast.3, bf16[128,128,128]{2,1,0:T(8,128)(2,1)} %a_hbm.1, bf16[4,128,128]{2,1,0:T(8,128)(2,1)} %p_hbm.1), custom_call_target="tpu_custom_call" | custom-call | tf_op jit(solution)/shard_map/pallas_call | solution.py:361
  73.5 1.5 %copy.8 = bf16[2,128,128]{2,1,0:T(8,128)(2,1)} copy(bf16[2,128,128]{2,1,0:T(8,128)(2,1)} %shard_map.55) | data formatting | bytes 131072

commit v3 on v2

--- a/solution.py
+++ b/solution.py
@@ -16,9 +16,10 @@
 
 def kernel_body(
     n_row, pb, slots, width,
-    acol_s, arow_s, acount_s, acol_v, arow_v, a_hbm, p_hbm, out_ref,
+    acol_h, arow_h, acount_h, a_hbm, p_hbm, out_ref,
     abuf, colbuf, row0, row1, img, seg0, seg1, tabv, tabs,
     fbuf, frecv, nbuf, nrecv, red, zb, zr,
+    acol_s, arow_s, acount_s, acol_v, arow_v, s_sem,
     a_sem, p_sem, t_sem, sh_send, sh_recv,
     z_send, z_recv, x_send, x_recv, y_send, y_recv,
     f_send, f_recv, n_send, n_recv, q_send, q_recv,
@@ -58,6 +59,10 @@
     own = colbuf.at[pl.ds(pb, pb)]
     p_copy = pltpu.make_async_copy(p_hbm, own, p_sem)
     p_copy.start()
+    small = [
+        pltpu.make_async_copy(src, dst, s_sem.at[i]) for i, (src, dst) in enumerate((
+            (acol_h, acol_s), (arow_h, arow_s), (acount_h, acount_s),
+            (acol_h, acol_v), (arow_h, arow_v)))]
     barrier = pltpu.get_barrier_semaphore()
     for dev in (right, left, mate):
         signal(dev)
@@ -76,13 +81,13 @@
 
     half = pb // 2
 
-    def z_msg(q, zz, dev):
-        s = rowb[q].at[pl.ds((x * NZ + zz) * pb, pb)]
-        return remote(s, s, z_send.at[q, zz], z_recv.at[q, zz], dev)
-
-    def z_both(q, side):
-        s = rowb[q].at[pl.ds(col * pb, pb)]
-        return remote(s, s, z_send.at[q, NZ + side], z_recv.at[q, z], zup if side == 0 else zdn)
+    def z_msg(q, zz, h, dev):
+        s = rowb[q].at[pl.ds((x * NZ + zz) * pb + h * half, half)]
+        return remote(s, s, z_send.at[q, h, zz], z_recv.at[q, h, zz], dev)
+
+    def z_both(q, side, h):
+        s = rowb[q].at[pl.ds(col * pb + h * half, half)]
+        return remote(s, s, z_send.at[q, h, NZ + side], z_recv.at[q, h, z], zup if side == 0 else zdn)
 
     def x_msg(q, d, xx, zz):
         s = rowb[q].at[pl.ds((xx * NZ + zz) * pb, pb)]
@@ -103,16 +108,15 @@
         return jnp.where(n <= 2 * pairs, side, rest)
 
     def step(q, n):
-        if n == 0:
-            pl.when(has_up)(lambda: z_both(q, 0).start())
-            pl.when(has_dn)(lambda: z_both(q, 1).start())
-            x_msg(q, 0, x, z).start()
-            x_msg(q, 1, x, z).start()
-            return
         zz = place(n)
-        z_msg(q, zz, zup).wait_recv()
-        pl.when((zz < z) & has_up)(lambda: z_msg(q, zz, zup).start())
-        pl.when((zz > z) & has_dn)(lambda: z_msg(q, zz, zdn).start())
+        for h in range(2):
+            if n == 0:
+                pl.when(has_up)(lambda h=h: z_both(q, 0, h).start())
+                pl.when(has_dn)(lambda h=h: z_both(q, 1, h).start())
+            else:
+                z_msg(q, zz, h, zup).wait_recv()
+                pl.when((zz < z) & has_up)(lambda h=h: z_msg(q, zz, h, zup).start())
+                pl.when((zz > z) & has_dn)(lambda h=h: z_msg(q, zz, h, zdn).start())
         x_msg(q, 0, x, zz).start()
         x_msg(q, 1, x, zz).start()
 
@@ -130,13 +134,14 @@
             y_msg(q, 1, xf, zz).wait_recv()
 
     def drain(q):
-        pl.when(has_up)(lambda: z_both(q, 0).wait_send())
-        pl.when(has_dn)(lambda: z_both(q, 1).wait_send())
+        for h in range(2):
+            pl.when(has_up)(lambda h=h: z_both(q, 0, h).wait_send())
+            pl.when(has_dn)(lambda h=h: z_both(q, 1, h).wait_send())
         for n in range(NZ):
             zz = place(n)
-            if n > 0:
-                pl.when((zz < z) & has_up)(lambda: z_msg(q, zz, zup).wait_send())
-                pl.when((zz > z) & has_dn)(lambda: z_msg(q, zz, zdn).wait_send())
+            for h in range(2 if n > 0 else 0):
+                pl.when((zz < z) & has_up)(lambda h=h, zz=zz: z_msg(q, zz, h, zup).wait_send())
+                pl.when((zz > z) & has_dn)(lambda h=h, zz=zz: z_msg(q, zz, h, zdn).wait_send())
             for d in range(2):
                 x_msg(q, d, x, zz).wait_send()
                 y_msg(q, d, x, zz).wait_send()
@@ -154,13 +159,15 @@
         pltpu.make_async_copy(
             a_hbm.at[pl.ds(i * part, part)], abuf.at[pl.ds(i * part, part)], a_sem.at[i])
         for i in range(n_a)]
-    for c in a_copies:
+    for c in small + a_copies:
         c.start()
 
+    for c in small:
+        c.wait()
     lane = lax.broadcasted_iota(I32, (slots, slots), 1)
     sub = lax.broadcasted_iota(I32, (slots, slots), 0)
-    acol = jnp.broadcast_to(acol_v[...], (slots, slots))
-    arow = jnp.broadcast_to(arow_v[...], (slots, slots))
+    acol = jnp.broadcast_to(acol_v[...].reshape(1, slots), (slots, slots))
+    arow = jnp.broadcast_to(arow_v[...].reshape(1, slots), (slots, slots))
     n_out = nc * pb
     key = jnp.where(lane < acount_s[0], (arow & (pb - 1)) * nc + acol, n_out)
     key_t = key.T
@@ -291,43 +298,33 @@
     to_far.wait_recv()
     for c in a_copies:
         c.wait()
-    images(0, 64)
-    relay(0, NZ - 2)
-    relay(1, NZ - 2)
-    images(64, 64)
-    relay(0, NZ - 1)
-    relay(1, NZ - 1)
+    quarter = slots // 4
+    for i, (n, q) in enumerate([(NZ - 2, 0), (NZ - 2, 1), (NZ - 1, 0), (NZ - 1, 1)]):
+        images(i * quarter, quarter)
+        relay(q, n)
     t_copy.wait()
     arrived(0)
     terms(0, 0, slots)
-    send_far(0, 0)
-    send_far(0, 1)
-    send_near(0, 0)
-    send_joint(0, 0)
-    send_far(0, 2)
-    send_near(0, 1)
-    send_joint(0, 1)
-    send_near(0, 2)
     arrived(1)
-    terms(1, 0, 64)
-    send_joint(0, 2)
-    terms(1, 64, 64)
-    send_far(1, 0)
-    send_far(1, 1)
-    send_near(1, 0)
-    finish(0, 0)
-    send_joint(1, 0)
-    finish(0, 1)
-    send_far(1, 2)
-    send_near(1, 1)
-    send_joint(1, 1)
-    finish(0, 2)
-    send_near(1, 2)
-    send_joint(1, 2)
-    finish(1, 0)
-    finish(1, 1)
-    finish(1, 2)
+    for i in range(NZ // 2):
+        send_far(0, i)
+    for i in range(NZ // 2):
+        send_near(0, i)
+    terms(1, 0, slots // 2)
+    for i in range(NZ // 2):
+        send_joint(0, i)
+    terms(1, slots // 2, slots // 2)
+    for i in range(NZ // 2):
+        send_far(1, i)
+    for i in range(NZ // 2):
+        send_near(1, i)
+    for i in range(NZ // 2):
+        finish(0, i)
+    for i in range(NZ // 2):
+        send_joint(1, i)
     close(0)
+    for i in range(NZ // 2):
+        finish(1, i)
     close(1)
 
     to_mate.wait_send()
@@ -354,14 +351,13 @@
     part = (width // NQ, width)
     vm = pltpu.VMEM
     dma = pltpu.SemaphoreType.DMA
-    smem = pl.BlockSpec(memory_space=pltpu.SMEM)
     vmem = pl.BlockSpec(memory_space=pltpu.VMEM)
-    hbm = pl.BlockSpec(memory_space=pl.ANY)
+    hbm = pl.BlockSpec(memory_space=pltpu.HBM)
     ng = NZ // 2
     return pl.pallas_call(
         functools.partial(kernel_body, n_row, pb, slots, width),
         out_shape=jax.ShapeDtypeStruct((ct,) + tile, BF16),
-        in_specs=[smem, smem, smem, vmem, vmem, hbm, hbm],
+        in_specs=[hbm] * 5,
         out_specs=vmem,
         scratch_shapes=[
             vm((slots,) + tile, BF16),
@@ -380,15 +376,17 @@
             vm((NQ, ct) + part, F32),
             vm((NQ, NZ, ct) + part, BF16),
             vm((NQ, NZ, ct) + part, BF16),
+            pltpu.SMEM((slots,), I32), pltpu.SMEM((slots,), I32), pltpu.SMEM((1,), I32),
+            vm((slots,), I32), vm((slots,), I32), dma((5,)),
             dma((4,)), dma(()), dma(()), dma((2,)), dma((2,)),
-            dma((NQ, NZ + 2)), dma((NQ, NZ)),
+            dma((NQ, 2, NZ + 2)), dma((NQ, 2, NZ)),
             dma((NQ, 2, NZ)), dma((NQ, 2, NZ)), dma((NQ, 2, NZ)), dma((NQ, 2, NZ)),
             dma((NQ, 2, ng)), dma((NQ, 2, ng)), dma((NQ, 2, NZ)), dma((NQ, 2, NZ)),
             dma((NQ, NZ)), dma((NQ, NZ)),
         ],
         compiler_params=pltpu.CompilerParams(
             collective_id=0, has_side_effects=True, vmem_limit_bytes=67043328),
-    )(a_col, a_row, a_count, a_col.reshape(1, slots), a_row.reshape(1, slots), a_tiles, p_tiles)
+    )(a_col, a_row, a_count, a_tiles, p_tiles)
 
 
 def solution(mesh):

time: 75.2 us -> 73.1 us (0.972)
  the two profiles are of different devices: /device:TPU:600 before, /device:TPU:64 now
where the time goes in v3:
time: 73.1 us; the launch traced here: 72.9 us
  Pallas kernels  70.7 us (97%)
  local copies, waits for them, and re-layouts  1.47 us (2%)
    pallas_call x1, Pallas kernels, shards(): pl.pallas_call(functools.partial(kernel_body, n_row, pb, slots, width), o...  70.7 us
    unnamed x1, local copies, waits for them, and re-layouts  1.47 us

profile of v3, /device:TPU:64, one launch (start us, length us, event | category | flops | bytes accessed | tf_op | source)
XLA Modules:
  0.0 72.9 jit_solution(12580177299064425443)
XLA Ops:
  0.7 70.7 %shard_map.55 = bf16[2,128,128]{2,1,0:T(8,128)(2,1)} custom-call(s32[128]{0:T(128)} %acol_h.1, s32[128]{0:T(128)} %arow_h.1, s32[1]{0:T(128)S(6)} %copy.7.acount_h, bf16[128,128,128]{2,1,0:T(8,128)(2,1)} %a_hbm.1, bf16[4,128,128]{2,1,0:T(8,128)(2,1)} %p_hbm.1), custom_call_target="tpu_custom_call" | custom-call | tf_op jit(solution)/shard_map/pallas_call | solution.py:357
  71.4 1.5 %copy.8 = bf16[2,128,128]{2,1,0:T(8,128)(2,1)} copy(bf16[2,128,128]{2,1,0:T(8,128)(2,1)} %shard_map.55) | data formatting | bytes 131072

commit v4 on v3

--- a/solution.py
+++ b/solution.py
@@ -192,7 +192,7 @@
     t_copy = pltpu.make_async_copy(tabv, tabs, t_sem)
     t_copy.start()
 
-    U = 8
+    U = 32
 
     def images(first, count):
         def body(i, carry):

time: 73.1 us -> 71.3 us (0.975)
  the two profiles are of different devices: /device:TPU:64 before, /device:TPU:2 now
where the time goes in v4:
time: 71.3 us; the launch traced here: 71.1 us
  Pallas kernels  69 us (97%)
  local copies, waits for them, and re-layouts  1.47 us (2%)
    pallas_call x1, Pallas kernels, shards(): pl.pallas_call(functools.partial(kernel_body, n_row, pb, slots, width), o...  69 us
    unnamed x1, local copies, waits for them, and re-layouts  1.47 us

profile of v4, /device:TPU:2, one launch (start us, length us, event | category | flops | bytes accessed | tf_op | source)
XLA Modules:
  0.0 71.1 jit_solution(473249421449872001)
XLA Ops:
  0.7 69.0 %shard_map.55 = bf16[2,128,128]{2,1,0:T(8,128)(2,1)} custom-call(s32[128]{0:T(128)} %acol_h.1, s32[128]{0:T(128)} %arow_h.1, s32[1]{0:T(128)S(6)} %copy.7.acount_h, bf16[128,128,128]{2,1,0:T(8,128)(2,1)} %a_hbm.1, bf16[4,128,128]{2,1,0:T(8,128)(2,1)} %p_hbm.1), custom_call_target="tpu_custom_call" | custom-call | tf_op jit(solution)/shard_map/pallas_call | solution.py:357
  69.6 1.5 %copy.8 = bf16[2,128,128]{2,1,0:T(8,128)(2,1)} copy(bf16[2,128,128]{2,1,0:T(8,128)(2,1)} %shard_map.55) | data formatting | bytes 131072

commit v5 on v4

--- a/solution.py
+++ b/solution.py
@@ -301,15 +301,18 @@
     quarter = slots // 4
     for i, (n, q) in enumerate([(NZ - 2, 0), (NZ - 2, 1), (NZ - 1, 0), (NZ - 1, 1)]):
         images(i * quarter, quarter)
-        relay(q, n)
+        if i < 3:
+            relay(q, n)
     t_copy.wait()
     arrived(0)
-    terms(0, 0, slots)
+    terms(0, 0, slots // 2)
+    relay(1, NZ - 1)
+    terms(0, slots // 2, slots // 2)
+    for i in range(NZ // 2):
+        send_far(0, i)
+    for i in range(NZ // 2):
+        send_near(0, i)
     arrived(1)
-    for i in range(NZ // 2):
-        send_far(0, i)
-    for i in range(NZ // 2):
-        send_near(0, i)
     terms(1, 0, slots // 2)
     for i in range(NZ // 2):
         send_joint(0, i)

time: 71.3 us -> 71.6 us (level)
  the two profiles are of different devices: /device:TPU:2 before, /device:TPU:64 now
where the time goes in v5:
time: 71.6 us; the launch traced here: 71.4 us
  Pallas kernels  69.3 us (97%)
  local copies, waits for them, and re-layouts  1.47 us (2%)
    pallas_call x1, Pallas kernels, shards(): pl.pallas_call(functools.partial(kernel_body, n_row, pb, slots, width), o...  69.3 us
    unnamed x1, local copies, waits for them, and re-layouts  1.47 us

profile of v5, /device:TPU:64, one launch (start us, length us, event | category | flops | bytes accessed | tf_op | source)
XLA Modules:
  0.0 71.4 jit_solution(9049425125314959205)
XLA Ops:
  0.7 69.3 %shard_map.55 = bf16[2,128,128]{2,1,0:T(8,128)(2,1)} custom-call(s32[128]{0:T(128)} %acol_h.1, s32[128]{0:T(128)} %arow_h.1, s32[1]{0:T(128)S(6)} %copy.7.acount_h, bf16[128,128,128]{2,1,0:T(8,128)(2,1)} %a_hbm.1, bf16[4,128,128]{2,1,0:T(8,128)(2,1)} %p_hbm.1), custom_call_target="tpu_custom_call" | custom-call | tf_op jit(solution)/shard_map/pallas_call | solution.py:360
  69.9 1.5 %copy.8 = bf16[2,128,128]{2,1,0:T(8,128)(2,1)} copy(bf16[2,128,128]{2,1,0:T(8,128)(2,1)} %shard_map.55) | data formatting | bytes 131072
